TPU v7x, 32 devices: a whole 2x2x4 slice. The times are simulated.
32 devices in a mesh: row: 8 (over y, x, core), col: 4 (over z).
Axes of the slice: x: 2, y: 2, z: 4, core: 2. Of those that a mesh axis runs over, the one named last changes fastest.
Arguments:
- panel: bfloat16 [24576, 256], P('row', 'col'), as said below
- trailing: bfloat16 [24576, 16384], P('row', 'col'), may hold values from -6 to 6
- tile_list: int32 [176], P('row'), may hold values from 0 to 23, as said below
Outputs:
- triangle: float32 [256, 256], replicated
- top_rows: float32 [16384, 256], P('col')
- updated: bfloat16 [22528, 16384], P('row', 'col')
Inputs may be any that keep to these rules, and one draw needn't show every extreme that they name: `tile_list`: each aligned block of 22 entries (the entries of one index of row) lists distinct tile numbers of that group's 24 tiles in increasing order and always includes tile 24 - 1. `panel`: the active rows of every row group, and all active rows together, have full column rank with a condition number under 100.
All inputs are finite; a program needn't handle non-finite values.
Results may differ from a plain program's by a relative error of at most 0.0065.
Values may be sent and summed in bfloat16 or wider, within the bound.
No kernel may reach another device: no remote copies, remote signals or barrier semaphores. Data moves between devices by JAX's collectives and lax.ppermute only.
A program may use at most 128 MiB of HBM per device.

v0:
```python
import jax
import jax.numpy as jnp
from jax import lax
from jax.sharding import PartitionSpec as P

TILE = 128


def pick_tiles(whole, tile_list):
    tiled = whole.reshape(-1, TILE, whole.shape[1])
    return jnp.take(tiled, tile_list, axis=0).reshape(-1, whole.shape[1])


def local(panel, trailing, tile_list):
    panel_full = lax.all_gather(panel, "col", axis=1, tiled=True)
    act_panel = pick_tiles(panel_full, tile_list)
    act_trail = pick_tiles(trailing, tile_list)
    local_gram = lax.dot_general(
        act_panel, act_panel, (((0,), (0,)), ((), ())), preferred_element_type=jnp.float32
    )
    gram_matrix = lax.psum(local_gram.astype(jnp.bfloat16), "row").astype(jnp.float32)
    lower_factor = jnp.linalg.cholesky(gram_matrix)
    triangle = lower_factor.T
    local_cross = lax.dot_general(
        act_trail, act_panel, (((0,), (0,)), ((), ())), preferred_element_type=jnp.float32
    )
    cross_sum = lax.psum(local_cross, "row")
    top_rows = jax.scipy.linalg.solve_triangular(lower_factor, cross_sum.T, lower=True).T
    coeff = jax.scipy.linalg.solve_triangular(
        lower_factor, top_rows.T, lower=True, trans=1
    ).T.astype(jnp.bfloat16)
    product = lax.dot_general(
        act_panel, coeff, (((1,), (1,)), ((), ())), preferred_element_type=jnp.float32
    )
    updated = (act_trail.astype(jnp.float32) - product).astype(jnp.bfloat16)
    return (triangle, top_rows, updated)


def solution(mesh):
    return jax.shard_map(
        local,
        mesh=mesh,
        in_specs=(P("row", "col"), P("row", "col"), P("row")),
        out_specs=(P(), P("col", None), P("row", "col")),
        check_vma=False,
    )
```

profile of v0, /device:TPU:0, one launch (start us, length us, event | category | flops | bytes accessed | tf_op | source)
XLA Modules:
  0.0 239.5 jit_solution(15465657170109536758)
XLA Ops:
  9.4 17.7 %gather_fusion.1 = bf16[22,128,4096]{2,1,0:T(8,128)(2,1)} fusion(bf16[24,128,4096]{2,1,0:T(8,128)(2,1)} %bitcast.57, s32[1024]{0:T(1024)S(1)} %pad_clamp_fusion), kind=kCustom, calls=%fused_computation.1 | custom fusion | bytes 46137432 | tf_op jit(solution)/shard_map/jit(_take)/gather | solution.py:11
  27.1 20.6 %bitcast_select_fusion = bf16[2816,4096]{1,0:T(8,128)(2,1)} fusion(bf16[22,128,4096]{2,1,0:T(8,128)(2,1)} %gather_fusion.1, pred[2816]{0:T(1024)(128)(4,1)S(1)} %broadcast_bitcast_fusion), kind=kLoop, calls=%fused_computation.5 | loop fusion | flops 11534336 | bytes 46140160 | tf_op jit(solution)/shard_map/jit(_take)/select_n | solution.py:11
  47.7 1.6 all-gather.2.cloned.1.call-done
  49.3 1.7 copy.11
  51.7 1.5 fusion.12
  53.2 12.2 %fusion.4 = f32[256,4096]{1,0:T(8,128)} fusion(bf16[22,128,4096]{2,1,0:T(8,128)(2,1)} %gather_fusion.1, pred[22]{0:T(512)(128)(4,1)S(1)} %compare_and_fusion, bf16[22,128,256]{2,1,0:T(8,128)(2,1)S(1)} %gather_fusion), kind=kOutput, calls=%fused_computation.10 | convolution fusion | flops 5917835264 | bytes 28704790 | tf_op jit(solution)/shard_map/dot_general | solution.py:24
  65.4 1.7 bitcast_select_fusion.1
  67.1 40.8 %all-reduce.4.cloned.1.call-done = bf16[256,256]{0,1:T(8,128)(2,1)} async-done(((bf16[256,256]{0,1:T(8,128)(2,1)}), bf16[256,256]{0,1:T(8,128)(2,1)}) %all-reduce.4.cloned.1.call-update) | async-done | bytes 131088 | tf_op jit(solution)/shard_map/psum | solution.py:21
  109.9 11.7 %cholesky.50 = f32[128,128]{1,0:T(8,128)S(1)} custom-call(f32[128,128]{1,0:T(8,128)S(1)} %cholesky.118), custom_call_target="Cholesky" | custom-call | tf_op jit(solution)/shard_map/jit(cholesky)/cholesky | solution.py:22
  121.6 9.8 %custom-call.18 = f32[1,128,128]{1,2,0:T(8,128)S(1)} custom-call(f32[1,128,128]{2,1,0:T(8,128)S(1)} %get-tuple-element.32), custom_call_target="InvertDiagBlocksLowerTriangular" | custom-call | tf_op jit(solution)/shard_map/jit(cholesky)/cholesky | solution.py:22
  131.9 11.7 %cholesky.105 = f32[128,128]{1,0:T(8,128)S(1)} custom-call(f32[128,128]{1,0:T(8,128)S(1)} %convolution_subtract_fusion.2), custom_call_target="Cholesky" | custom-call | tf_op jit(solution)/shard_map/jit(cholesky)/cholesky | solution.py:22
  146.6 4.0 %while.1 = (s32[]{:T(128)}, f32[256,256]{1,0:T(8,128)S(1)}, s32[2,2]{1,0:T(2,128)S(1)}, f32[2,128,128]{2,1,0:T(8,128)S(1)}, s32[]{:T(128)}) while((s32[]{:T(128)}, f32[256,256]{1,0:T(8,128)S(1)}, s32[2,2]{1,0:T(2,128)S(1)}, f32[2,128,128]{2,1,0:T(8,128)S(1)}, s32[]{:T(128)}) %tuple.31), condition=%wide.while_cond, body=%wide.while_body.sunk | while | flops 2 | bytes 131189 | solution.py:28
  147.2 1.4 bitcast_dynamic-update-slice_fusion.2
  150.6 19.9 %custom-call.19 = f32[2,128,128]{1,2,0:T(8,128)S(1)} custom-call(f32[2,128,128]{2,1,0:T(8,128)S(1)} %get-tuple-element.10), custom_call_target="InvertDiagBlocksLowerTriangular" | custom-call | tf_op jit(solution)/shard_map/jit(_solve_triangular)/triangular_solve | solution.py:28
  170.5 21.7 %all-reduce.6.cloned.1.call-done = f32[256,4096]{1,0:T(8,128)} async-done(((f32[256,4096]{1,0:T(8,128)}), f32[256,4096]{1,0:T(8,128)}) %all-reduce.6.cloned.1.call-update) | async-done | bytes 4194320 | tf_op jit(solution)/shard_map/psum | solution.py:27
  192.2 3.6 %fusion.7 = f32[128,4096]{1,0:T(8,128)S(1)} fusion(f32[256,4096]{1,0:T(8,128)} %all-reduce.6.cloned.1.call-done, f32[2,128,128]{1,2,0:T(8,128)S(1)} %custom-call.19), kind=kOutput, calls=%fused_computation.15 | convolution fusion | flops 805306368 | bytes 4259840 | tf_op jit(solution)/shard_map/jit(_solve_triangular)/triangular_solve | solution.py:28
  195.9 1.9 convolution_subtract_fusion.1
  197.8 1.9 fusion.20
  199.8 1.9 fusion.27
  201.7 2.5 %maximum_bitcast_fusion = f32[4096,256]{0,1:T(8,128)} fusion(f32[128,4096]{1,0:T(8,128)S(1)} %fusion.20, f32[128,4096]{1,0:T(8,128)S(1)} %fusion.7), kind=kLoop, calls=%fused_computation.14 | loop fusion | flops 1048576 | bytes 8388608 | tf_op jit(solution)/shard_map/transpose | solution.py:28
  204.2 2.0 convolution_subtract_fusion
  206.2 1.9 convolution_convert_fusion
  208.1 5.9 %copy.17 = f32[4096,256]{1,0:T(8,128)} copy(f32[4096,256]{0,1:T(8,128)} %maximum_bitcast_fusion) | data formatting | bytes 8388608
  213.9 19.1 %subtract_convert_fusion = bf16[2816,4096]{1,0:T(8,128)(2,1)} fusion(bf16[2816,4096]{1,0:T(8,128)(2,1)} %bitcast_select_fusion, bf16[2816,256]{1,0:T(8,128)(2,1)S(1)} %bitcast_select_fusion.1, bf16[128,4096]{1,0:T(8,128)(2,1)S(1)} %get-tuple-element.35, bf16[128,4096]{1,0:T(8,128)(2,1)S(1)} %convolution_convert_fusion), kind=kOutput, calls=%fused_computation.4 | convolution fusion | flops 5944377344 | bytes 49676288 | tf_op jit(solution)/shard_map/dot_general | solution.py:32
  (36 shorter events, 9.6 us)
Async XLA Ops:
  7.2 42.2 %all-gather.2.cloned.1.call-start = ((), (), s32[]{:S(2)}) async-start(), calls=%async_computation | async-start | bytes 1966080 | tf_op jit(solution)/shard_map/all_gather | solution.py:15
  7.9 100.0 %all-reduce.4.cloned.1.call-start = ((), (), s32[]{:S(2)}) async-start(), calls=%async_computation.1 | async-start | bytes 262144 | tf_op jit(solution)/shard_map/psum | solution.py:21
  53.2 139.0 %all-reduce.6.cloned.1.call-start = ((), (), s32[]{:S(2)}) async-start(), calls=%async_computation.2 | async-start | bytes 8388608 | tf_op jit(solution)/shard_map/psum | solution.py:27
  170.5 29.2 %copy-start.1 = (f32[2,128,128]{1,2,0:T(8,128)}, f32[2,128,128]{1,2,0:T(8,128)S(1)}, u32[]{:S(2)}) copy-start(f32[2,128,128]{1,2,0:T(8,128)S(1)} %custom-call.19) | copy-start | bytes 393220
  192.2 3.7 %copy-start = (f32[256,4096]{1,0:T(8,128)S(1)}, f32[256,4096]{1,0:T(8,128)}, u32[]{:S(2)}) copy-start(f32[256,4096]{1,0:T(8,128)} %all-reduce.6.cloned.1.call-done) | copy-start | bytes 12582916
  204.2 2.0 copy-start.2
Sparse Core Ops, SparseCore 0:
  9.5 39.7 all-gather.1
  53.3 54.5 all-reduce.3
  111.7 80.4 all-reduce.5
where the time goes:
time: 240 us
  other arithmetic  80.9 us (34%)
  waiting for transfers between devices  64.8 us (27%)
  matrix products  46.5 us (19%)
  local copies, waits for them, and re-layouts  31.9 us (13%)
  between operations  15.2 us (6%)
    psum x1, waiting for transfers between devices, local(): lax.psum(local_gram.astype(jnp.bfloat16), 'row').astype(jnp.float32)  40.8 us
    another operation x6, other arithmetic, local(): lower_factor = jnp.linalg.cholesky(gram_matrix)  34 us
    select_n x3, other arithmetic, pick_tiles(): return jnp.take(tiled, tile_list, axis=0).reshape(-1, whole.shape[1])  22.9 us
    psum x1, waiting for transfers between devices, local(): cross_sum = lax.psum(local_cross, 'row')  21.7 us
    another operation x3, other arithmetic, local(): jax.scipy.linalg.solve_triangular(lower_factor, cross_sum.T, lower=True)  19.9 us
    dot_general x1, matrix products, local(): lax.dot_general(act_panel, coeff, (((1,), (1,)), ((), ())), preferred_ele...  19.1 us
    gather x2, local copies, waits for them, and re-layouts, pick_tiles(): return jnp.take(tiled, tile_list, axis=0).reshape(-1, whole.shape[1])  18.4 us
    dot_general x1, matrix products, local(): lax.dot_general(act_trail, act_panel, (((0,), (0,)), ((), ())), preferred...  12.2 us
  transfers between devices with their start and end apart: 3, of which 3 were waited for; matrix products, arithmetic and copies ran while one was open for 48% of the time, Pallas kernels for 0%

commit v1 on v0

--- a/solution.py
+++ b/solution.py
@@ -24,7 +24,11 @@
     local_cross = lax.dot_general(
         act_trail, act_panel, (((0,), (0,)), ((), ())), preferred_element_type=jnp.float32
     )
-    cross_sum = lax.psum(local_cross, "row")
+    cross_sum = local_cross
+    for hop in (1, 2, 4):
+        cross_sum = cross_sum + lax.ppermute(
+            cross_sum, "row", [(dev, dev ^ hop) for dev in range(8)]
+        )
     top_rows = jax.scipy.linalg.solve_triangular(lower_factor, cross_sum.T, lower=True).T
     coeff = jax.scipy.linalg.solve_triangular(
         lower_factor, top_rows.T, lower=True, trans=1

time: 240 us -> 363 us (1.51); the launches traced: 240 us -> 356 us
  waiting for transfers between devices: 64.8 us -> 172 us
  other arithmetic: 80.9 us -> 87.4 us
    ppermute x0 -> x3, waiting for transfers between devices: none -> 98.2 us  [local(): lax.ppermute(cross_sum, 'row', [(dev, dev ^ hop) for dev in range(8)])]
    psum x1 -> x0, waiting for transfers between devices: 21.7 us -> none  [local(): cross_sum = lax.psum(local_cross, 'row')]
    all_gather x1, waiting for transfers between devices: 1.63 us -> 23 us  [local(): panel_full = lax.all_gather(panel, 'col', axis=1, tiled=True)]
    psum x1, waiting for transfers between devices: 40.8 us -> 49.8 us  [local(): lax.psum(local_gram.astype(jnp.bfloat16), 'row').astype(jnp.float32)]
    transpose x0 -> x1, other arithmetic: none -> 4.04 us  [local(): top_rows = jax.scipy.linalg.solve_triangular(lower_factor, cross_sum.T, l...]
  transfers between devices with their start and end apart: 3 -> 5, of which waited for: 3 -> 4; matrix products, arithmetic and copies ran while one was open for 48% -> 29% of each run, Pallas kernels for 0% -> 0%
where the time goes in v1:
time: 363 us; the launch traced here: 356 us
  waiting for transfers between devices  172 us (47%)
  other arithmetic  87.4 us (24%)
  matrix products  46.4 us (13%)
  local copies, waits for them, and re-layouts  31.5 us (9%)
  between operations  15.8 us (4%)
    ppermute x3, waiting for transfers between devices, local(): lax.ppermute(cross_sum, 'row', [(dev, dev ^ hop) for dev in range(8)])  98.2 us
    psum x1, waiting for transfers between devices, local(): lax.psum(local_gram.astype(jnp.bfloat16), 'row').astype(jnp.float32)  49.8 us
    another operation x6, other arithmetic, local(): lower_factor = jnp.linalg.cholesky(gram_matrix)  34 us
    select_n x3, other arithmetic, pick_tiles(): return jnp.take(tiled, tile_list, axis=0).reshape(-1, whole.shape[1])  23.2 us
    all_gather x1, waiting for transfers between devices, local(): panel_full = lax.all_gather(panel, 'col', axis=1, tiled=True)  23 us
    another operation x3, other arithmetic, local(): jax.scipy.linalg.solve_triangular(lower_factor, cross_sum.T, lower=True)  19.9 us
    dot_general x1, matrix products, local(): lax.dot_general(act_panel, coeff, (((1,), (1,)), ((), ())), preferred_ele...  19.1 us
    gather x2, local copies, waits for them, and re-layouts, pick_tiles(): return jnp.take(tiled, tile_list, axis=0).reshape(-1, whole.shape[1])  18.4 us
  transfers between devices with their start and end apart: 5, of which 4 were waited for; matrix products, arithmetic and copies ran while one was open for 29% of the time, Pallas kernels for 0%

profile of v1, /device:TPU:0, one launch (start us, length us, event | category | flops | bytes accessed | tf_op | source)
XLA Modules:
  0.0 355.9 jit_solution(15178598162428567197)
XLA Ops:
  8.6 17.7 %gather_fusion.1 = bf16[22,128,4096]{2,1,0:T(8,128)(2,1)} fusion(bf16[24,128,4096]{2,1,0:T(8,128)(2,1)} %bitcast.58, s32[1024]{0:T(1024)S(1)} %pad_clamp_fusion), kind=kCustom, calls=%fused_computation.1 | custom fusion | bytes 46137432 | tf_op jit(solution)/shard_map/jit(_take)/gather | solution.py:11
  26.4 23.0 %all-gather.2.cloned.1.call-done = bf16[3072,256]{0,1:T(8,128)(2,1)} async-done(((bf16[3072,64]{0,1:T(8,128)(2,1)}), bf16[3072,256]{0,1:T(8,128)(2,1)}) %all-gather.2.cloned.1.call-update) | async-done | bytes 1572880 | tf_op jit(solution)/shard_map/all_gather | solution.py:15
  51.7 11.9 %fusion.4 = f32[4096,256]{1,0:T(8,128)S(1)} fusion(bf16[22,128,4096]{2,1,0:T(8,128)(2,1)} %gather_fusion.1, pred[22]{0:T(512)(128)(4,1)S(1)} %compare_and_fusion, bf16[22,128,256]{2,1,0:T(8,128)(2,1)S(1)} %gather_fusion), kind=kOutput, calls=%fused_computation.10 | convolution fusion | flops 5917835264 | bytes 28704790 | tf_op jit(solution)/shard_map/dot_general | solution.py:24
  63.6 7.1 %collective-permute-done = f32[4096,256]{1,0:T(8,128)S(1)} collective-permute-done((f32[4096,256]{1,0:T(8,128)S(1)}, f32[4096,256]{1,0:T(8,128)S(1)}, u32[]{:S(2)}, u32[]{:S(2)}) %collective-permute-start) | collective-permute-done | bytes 4194336 | tf_op jit(solution)/shard_map/ppermute | solution.py:29
  72.9 91.1 %collective-permute-done.1 = f32[4096,256]{1,0:T(8,128)S(1)} collective-permute-done((f32[4096,256]{1,0:T(8,128)S(1)}, f32[4096,256]{1,0:T(8,128)S(1)}, u32[]{:S(2)}, u32[]{:S(2)}) %collective-permute-start.1) | collective-permute-done | bytes 4194336 | tf_op jit(solution)/shard_map/ppermute | solution.py:29
  164.0 2.6 add.46
  168.0 20.6 %bitcast_select_fusion = bf16[2816,4096]{1,0:T(8,128)(2,1)} fusion(bf16[22,128,4096]{2,1,0:T(8,128)(2,1)} %gather_fusion.1, pred[2816]{0:T(1024)(128)(4,1)S(1)} %broadcast_bitcast_fusion), kind=kLoop, calls=%fused_computation.5 | loop fusion | flops 11534336 | bytes 46140160 | tf_op jit(solution)/shard_map/jit(_take)/select_n | solution.py:11
  190.1 1.9 bitcast_select_fusion.1
  192.0 49.8 %all-reduce.3.cloned.1.call-done = bf16[256,256]{0,1:T(8,128)(2,1)} async-done(((bf16[256,256]{0,1:T(8,128)(2,1)}), bf16[256,256]{0,1:T(8,128)(2,1)}) %all-reduce.3.cloned.1.call-update) | async-done | bytes 131088 | tf_op jit(solution)/shard_map/psum | solution.py:21
  243.8 11.7 %cholesky.50 = f32[128,128]{1,0:T(8,128)S(1)} custom-call(f32[128,128]{1,0:T(8,128)S(1)} %cholesky.118), custom_call_target="Cholesky" | custom-call | tf_op jit(solution)/shard_map/jit(cholesky)/cholesky | solution.py:22
  255.5 9.8 %custom-call.18 = f32[1,128,128]{1,2,0:T(8,128)S(1)} custom-call(f32[1,128,128]{2,1,0:T(8,128)S(1)} %get-tuple-element.32), custom_call_target="InvertDiagBlocksLowerTriangular" | custom-call | tf_op jit(solution)/shard_map/jit(cholesky)/cholesky | solution.py:22
  265.8 11.7 %cholesky.105 = f32[128,128]{1,0:T(8,128)S(1)} custom-call(f32[128,128]{1,0:T(8,128)S(1)} %convolution_subtract_fusion.1), custom_call_target="Cholesky" | custom-call | tf_op jit(solution)/shard_map/jit(cholesky)/cholesky | solution.py:22
  280.5 3.8 %while.1 = (s32[]{:T(128)}, f32[256,256]{1,0:T(8,128)S(1)}, s32[2,2]{1,0:T(2,128)S(1)}, f32[2,128,128]{2,1,0:T(8,128)S(1)}, s32[]{:T(128)}) while((s32[]{:T(128)}, f32[256,256]{1,0:T(8,128)S(1)}, s32[2,2]{1,0:T(2,128)S(1)}, f32[2,128,128]{2,1,0:T(8,128)S(1)}, s32[]{:T(128)}) %tuple.31), condition=%wide.while_cond, body=%wide.while_body.sunk | while | flops 2 | bytes 131189 | solution.py:32
  284.3 19.8 %custom-call.19 = f32[2,128,128]{1,2,0:T(8,128)S(1)} custom-call(f32[2,128,128]{2,1,0:T(8,128)S(1)} %get-tuple-element.10), custom_call_target="InvertDiagBlocksLowerTriangular" | custom-call | tf_op jit(solution)/shard_map/jit(_solve_triangular)/triangular_solve | solution.py:32
  304.2 4.0 %add_bitcast_fusion = f32[256,4096]{0,1:T(8,128)S(1)} fusion(f32[4096,256]{1,0:T(8,128)} %add.46, f32[4096,256]{1,0:T(8,128)} %collective-permute-done.2), kind=kLoop, calls=%fused_computation.14 | loop fusion | flops 1048576 | bytes 12582912 | tf_op jit(solution)/shard_map/transpose | solution.py:32
  308.2 2.0 fusion.8
  310.2 3.4 fusion.22
  313.7 2.1 fusion.7
  315.7 1.9 fusion.28
  317.6 2.4 maximum_bitcast_fusion
  320.0 2.2 convolution_subtract_fusion
  322.2 1.9 convolution_convert_fusion
  324.1 5.6 %copy.18 = f32[4096,256]{1,0:T(8,128)} copy(f32[4096,256]{0,1:T(8,128)} %maximum_bitcast_fusion) | data formatting | bytes 8388608
  329.7 19.1 %subtract_convert_fusion = bf16[2816,4096]{1,0:T(8,128)(2,1)} fusion(bf16[2816,4096]{1,0:T(8,128)(2,1)} %bitcast_select_fusion, bf16[2816,256]{1,0:T(8,128)(2,1)S(1)} %bitcast_select_fusion.1, bf16[128,4096]{1,0:T(8,128)(2,1)S(1)} %get-tuple-element.35, bf16[128,4096]{1,0:T(8,128)(2,1)S(1)} %convolution_convert_fusion), kind=kOutput, calls=%fused_computation.4 | convolution fusion | flops 5944377344 | bytes 49676288 | tf_op jit(solution)/shard_map/dot_general | solution.py:36
  (42 shorter events, 16.8 us)
Async XLA Ops:
  7.2 42.2 %all-gather.2.cloned.1.call-start = ((), (), s32[]{:S(2)}) async-start(), calls=%async_computation | async-start | bytes 1966080 | tf_op jit(solution)/shard_map/all_gather | solution.py:15
  7.9 233.9 %all-reduce.3.cloned.1.call-start = ((), (), s32[]{:S(2)}) async-start(), calls=%async_computation.1 | async-start | bytes 262144 | tf_op jit(solution)/shard_map/psum | solution.py:21
  8.6 17.7 %copy-start.2 = (s32[22]{0:T(128)S(1)}, s32[22]{0:T(128)}, u32[]{:S(2)}) copy-start(s32[22]{0:T(128)} %param.5) | copy-start | bytes 268
  63.5 7.2 %collective-permute-start = (f32[4096,256]{1,0:T(8,128)S(1)}, f32[4096,256]{1,0:T(8,128)S(1)}, u32[]{:S(2)}, u32[]{:S(2)}) collective-permute-start(f32[4096,256]{1,0:T(8,128)S(1)} %fusion.4), channel_id=1, source_target_pairs={{0,4},{4,0},{8,12},{12,8},{16,20},{20,16},{24,28},{28,24},{1,5},{5... | collective-permute-start | bytes 12582920 | tf_op jit(solution)/shard_map/ppermute | solution.py:29
  71.3 92.7 %collective-permute-start.1 = (f32[4096,256]{1,0:T(8,128)S(1)}, f32[4096,256]{1,0:T(8,128)S(1)}, u32[]{:S(2)}, u32[]{:S(2)}) collective-permute-start(f32[4096,256]{1,0:T(8,128)S(1)} %add.45), channel_id=1, source_target_pairs={{0,8},{4,12},{8,0},{12,4},{16,24},{20,28},{24,16},{28,20},{1,9},{5... | collective-permute-start | bytes 12582920 | tf_op jit(solution)/shard_map/ppermute | solution.py:29
  166.5 137.6 %collective-permute-start.2 = (f32[4096,256]{1,0:T(8,128)}, f32[4096,256]{1,0:T(8,128)}, u32[]{:S(2)}, u32[]{:S(2)}) collective-permute-start(f32[4096,256]{1,0:T(8,128)} %add.46), channel_id=1, source_target_pairs={{0,16},{4,20},{8,24},{12,28},{16,0},{20,4},{24,8},{28,12},{1,17},{... | collective-permute-start | bytes 12582920 | tf_op jit(solution)/shard_map/ppermute | solution.py:29
  304.2 11.6 %copy-start = (f32[2,128,128]{1,2,0:T(8,128)}, f32[2,128,128]{1,2,0:T(8,128)S(1)}, u32[]{:S(2)}) copy-start(f32[2,128,128]{1,2,0:T(8,128)S(1)} %custom-call.19) | copy-start | bytes 393220
  320.0 2.2 copy-start.1
Sparse Core Ops, SparseCore 0:
  9.5 39.7 all-gather.1
  190.2 51.5 all-reduce.2
